TPU v7x, 256 devices: a whole 4x4x8 slice. The times are simulated.
256 devices in a mesh: expert: 64 (over z, y, core), dp: 4 (over x).
Axes of the slice: x: 4, y: 4, z: 8, core: 2. Of those that a mesh axis runs over, the one named last changes fastest.
Arguments:
- prenorm_input: bfloat16 [32768, 1280], P(('expert', 'dp')), may hold values from -6 to 6
- gain: float32 [1280], replicated, may hold values from 0.25 to 1.75
- router: bfloat16 [1280, 32], replicated, may hold values from -0.15625 to 0.15625
- routes: int32 [32768, 2], P(('expert', 'dp')), may hold values from 0 to 31, all different within a row; in each aligned block of 128 rows (0 to 127, 128 to 255, ...) at most 10 rows name the same one
- w_in: bfloat16 [64, 1280, 1280], P('expert', None, 'dp'), may hold values from -0.15625 to 0.15625
- w_out: bfloat16 [64, 1280, 1280], P('expert', 'dp'), may hold values from -0.125 to 0.125
- cotangent: bfloat16 [32768, 1280], P(('expert', 'dp')), may hold values from -18 to 18
Outputs:
- input_grad: bfloat16 [32768, 1280], P(('expert', 'dp'))
- grad_in: bfloat16 [64, 1280, 1280], P('expert', None, 'dp')
- grad_out: bfloat16 [64, 1280, 1280], P('expert', 'dp')
- grad_router: float32 [1280, 32], replicated
- grad_gain: float32 [1280], replicated
Inputs may be any that keep to these rules, and one draw needn't show every extreme that they name: `routes`: each row names 2 different experts; among the rows of one device no expert is named more than 10 times.
All inputs are finite; a program needn't handle non-finite values.
Results may differ from a plain program's by a relative error of at most 0.015.
Values may be sent and summed in bfloat16 or wider, within the bound.
A program may use at most 128 MiB of HBM per device.

v0:
```python
import math
import jax
import jax.numpy as jnp
from jax import lax
from jax.sharding import PartitionSpec as P


def gelu_parts(pre):
    coeff = math.sqrt(2.0 / math.pi)
    inner = coeff * (pre + 0.044715 * pre * pre * pre)
    tanh_val = jnp.tanh(inner)
    value = 0.5 * pre * (1.0 + tanh_val)
    slope = 0.5 * (1.0 + tanh_val) + 0.5 * pre * (1.0 - tanh_val * tanh_val) * coeff * (
        1.0 + 3.0 * 0.044715 * pre * pre
    )
    return (value, slope)


def norm_pieces(block, gain):
    values = block.astype(jnp.float32)
    centred_rows = values - jnp.mean(values, axis=1, keepdims=True)
    inverse_deviation = lax.rsqrt(
        jnp.mean(centred_rows * centred_rows, axis=1, keepdims=True) + 1e-06
    )
    normalized_rows = centred_rows * inverse_deviation
    return (
        normalized_rows,
        inverse_deviation,
        (normalized_rows * gain[None, :]).astype(jnp.bfloat16),
    )


def slot_index(routing_rows, expert_list, expert_capacity):
    flat = routing_rows.reshape(-1)
    onehot = (flat[:, None] == jnp.arange(expert_list, dtype=jnp.int32)[None, :]).astype(jnp.int32)
    before = jnp.cumsum(onehot, axis=0) - onehot
    slot = jnp.sum(before * onehot, axis=1)
    return flat * expert_capacity + slot


def expert_pass(rows_m, rows_d, column, w_first, w_second):
    gate = jax.nn.sigmoid(jnp.dot(rows_m, column, preferred_element_type=jnp.float32)[:, 0])
    pre = jnp.dot(rows_m, w_first, preferred_element_type=jnp.float32)
    value, slope = gelu_parts(pre)
    hidden = value.astype(jnp.bfloat16)
    back = jnp.dot(rows_d, w_second.T, preferred_element_type=jnp.float32)
    gate_gradient = jnp.sum(hidden.astype(jnp.float32) * back, axis=1)
    grad_pre = (gate[:, None] * back * slope).astype(jnp.bfloat16)
    grad_y = (gate[:, None] * rows_d.astype(jnp.float32)).astype(jnp.bfloat16)
    grad_second = jnp.dot(hidden.T, grad_y, preferred_element_type=jnp.float32)
    grad_first = jnp.dot(rows_m.T, grad_pre, preferred_element_type=jnp.float32)
    row_gradient = jnp.dot(grad_pre, w_first.T, preferred_element_type=jnp.float32)
    return (row_gradient, gate_gradient, grad_first, grad_second)


def body(prenorm_input, gain, router, routes, w_in, w_out, cotangent):
    halves = lax.axis_size("expert")
    expert_list = halves // 2
    groups = lax.axis_size("dp")
    tok_rows = prenorm_input.shape[0]
    top = routes.shape[1]
    width = prenorm_input.shape[1]
    expert_capacity = max(2, 5 * tok_rows * top // (4 * expert_list))
    slots = expert_list * expert_capacity
    hi = lax.Precision.HIGHEST
    normalized_rows, inverse_deviation, mixed_rows = norm_pieces(prenorm_input, gain)
    where = slot_index(routes, expert_list, expert_capacity)
    places = (where[None, :] == jnp.arange(slots, dtype=jnp.int32)[:, None]).astype(jnp.bfloat16)
    send_m = jnp.dot(
        places, jnp.repeat(mixed_rows, top, axis=0), preferred_element_type=jnp.float32
    ).astype(jnp.bfloat16)
    send_d = jnp.dot(
        places, jnp.repeat(cotangent, top, axis=0), preferred_element_type=jnp.float32
    ).astype(jnp.bfloat16)
    send_m = jnp.repeat(send_m.reshape(expert_list, expert_capacity, width), 2, axis=0)
    send_d = jnp.repeat(send_d.reshape(expert_list, expert_capacity, width), 2, axis=0)
    recv_m, recv_d = (
        lax.all_to_all(send_m, "expert", split_axis=0, concat_axis=0, tiled=True),
        lax.all_to_all(send_d, "expert", split_axis=0, concat_axis=0, tiled=True),
    )
    own = lax.axis_index("expert") // 2
    column = lax.dynamic_slice_in_dim(router, own, 1, 1)
    all_m, all_d = (
        lax.all_gather(recv_m[None], "dp", axis=0, tiled=True),
        lax.all_gather(recv_d[None], "dp", axis=0, tiled=True),
    )
    row_gradient, gate_gradient, grad_first, grad_second = expert_pass(
        all_m.reshape(-1, width), all_d.reshape(-1, width), column, w_in[0], w_out[0]
    )
    summed_rows, summed_gate = (
        lax.psum_scatter(
            row_gradient.reshape(groups, halves * expert_capacity, width).astype(jnp.bfloat16),
            "dp",
            scatter_dimension=0,
            tiled=True,
        ).astype(jnp.float32),
        lax.psum_scatter(
            gate_gradient.reshape(groups, halves * expert_capacity).astype(jnp.bfloat16),
            "dp",
            scatter_dimension=0,
            tiled=True,
        ).astype(jnp.float32),
    )
    back_rows = summed_rows[0].reshape(halves, expert_capacity, width)
    back_gate = summed_gate[0].reshape(halves, expert_capacity)
    grad_in = grad_first[None].astype(jnp.bfloat16)
    grad_out = grad_second[None].astype(jnp.bfloat16)
    ret_rows, ret_gate = (
        lax.all_to_all(
            back_rows.astype(jnp.bfloat16), "expert", split_axis=0, concat_axis=0, tiled=True
        ).astype(back_rows.dtype),
        lax.all_to_all(
            back_gate.astype(jnp.bfloat16), "expert", split_axis=0, concat_axis=0, tiled=True
        ).astype(back_gate.dtype),
    )
    pair_rows = jnp.sum(ret_rows.reshape(expert_list, 2, expert_capacity, width), axis=1).reshape(
        slots, width
    )
    pair_gate = jnp.sum(ret_gate.reshape(expert_list, 2, expert_capacity), axis=1).reshape(slots)
    grad_expert = jnp.sum(jnp.take(pair_rows, where, axis=0).reshape(tok_rows, top, width), axis=1)
    dgate_tok = jnp.take(pair_gate, where, axis=0).reshape(tok_rows, top)
    logits = jnp.dot(mixed_rows, router, preferred_element_type=jnp.float32)
    choose = (routes[:, :, None] == jnp.arange(expert_list, dtype=jnp.int32)[None, None, :]).astype(
        jnp.float32
    )
    gates = jax.nn.sigmoid(jnp.sum(choose * logits[:, None, :], axis=2))
    dlogit = jnp.sum(choose * (dgate_tok * gates * (1.0 - gates))[:, :, None], axis=1)
    mixed_gradient = grad_expert + jnp.dot(dlogit, router.astype(jnp.float32).T, precision=hi)
    router_term = jnp.dot(mixed_rows.astype(jnp.float32).T, dlogit, precision=hi)
    gain_product = jnp.sum(mixed_gradient * normalized_rows, axis=0)
    grad_router, grad_gain = lax.psum((router_term, gain_product), ("expert", "dp"))
    scaled_rows = mixed_gradient * gain[None, :]
    mean_first_term = jnp.mean(scaled_rows, axis=1, keepdims=True)
    mean_second_term = jnp.mean(scaled_rows * normalized_rows, axis=1, keepdims=True)
    norm_backward = inverse_deviation * (
        scaled_rows - mean_first_term - normalized_rows * mean_second_term
    )
    input_grad = (cotangent.astype(jnp.float32) + norm_backward).astype(jnp.bfloat16)
    return (input_grad, grad_in, grad_out, grad_router, grad_gain)


def solution(mesh):
    in_specs = (
        P(("expert", "dp"), None),
        P(),
        P(),
        P(("expert", "dp"), None),
        P("expert", None, "dp"),
        P("expert", "dp", None),
        P(("expert", "dp"), None),
    )
    out_specs = (
        P(("expert", "dp"), None),
        P("expert", None, "dp"),
        P("expert", "dp", None),
        P(),
        P(),
    )
    return jax.shard_map(body, mesh=mesh, in_specs=in_specs, out_specs=out_specs, check_vma=False)
```

profile of v0, /device:TPU:1, one launch (start us, length us, event | category | flops | bytes accessed | tf_op | source)
XLA Modules:
  0.0 642.1 jit_solution(16606466589608056609)
XLA Ops:
  15.1 75.7 %all_to_all.21 = bf16[64,10,1280]{2,1,0:T(8,128)(2,1)S(1)} all-to-all(bf16[64,10,1280]{2,1,0:T(8,128)(2,1)S(1)} %bitcast.60), channel_id=1, replica_groups=mesh['expert'=64,'dp'=4] {'expert'}, dimensions={0} | all-to-all | bytes 3276800 | tf_op jit(solution)/shard_map/all_to_all | solution.py:78
  90.8 1.7 copy.53
  94.1 68.1 %all_to_all.22 = bf16[64,10,1280]{2,1,0:T(8,128)(2,1)S(1)} all-to-all(bf16[64,10,1280]{2,1,0:T(8,128)(2,1)S(1)} %bitcast.61), channel_id=1, replica_groups=mesh['expert'=64,'dp'=4] {'expert'}, dimensions={0} | all-to-all | bytes 3276800 | tf_op jit(solution)/shard_map/all_to_all | solution.py:79
  162.2 1.6 copy.55
  163.9 11.2 %copy.54 = bf16[256,10,1280]{2,1,0:T(8,128)(2,1)} copy(bf16[256,10,1280]{2,0,1:T(8,128)(2,1)} %all-gather.5.cloned.1.call-done) | data formatting | bytes 13107200 | tf_op jit(solution)/shard_map/all_gather | solution.py:84
  175.2 13.0 %reshape.183 = bf16[2560,1280]{1,0:T(8,128)(2,1)} reshape(bf16[256,10,1280]{2,1,0:T(8,128)(2,1)} %copy.54) | data formatting | bytes 13107200 | tf_op jit(solution)/shard_map/reshape | solution.py:88
  188.2 4.9 convolution_reduce_fusion
  193.2 4.1 fusion.15
  197.2 34.7 %all-gather.7.cloned.1.call-done = bf16[256,10,1280]{2,0,1:T(8,128)(2,1)} async-done(((bf16[64,10,1280]{2,0,1:T(8,128)(2,1)}), bf16[256,10,1280]{2,0,1:T(8,128)(2,1)}) %all-gather.7.cloned.1.call-update) | async-done | bytes 6553616 | tf_op jit(solution)/shard_map/all_gather | solution.py:85
  231.9 10.8 %copy.56 = bf16[256,10,1280]{2,1,0:T(8,128)(2,1)} copy(bf16[256,10,1280]{2,0,1:T(8,128)(2,1)} %all-gather.7.cloned.1.call-done) | data formatting | bytes 13107200 | tf_op jit(solution)/shard_map/all_gather | solution.py:85
  242.8 12.8 %reshape.188 = bf16[2560,1280]{1,0:T(8,128)(2,1)} reshape(bf16[256,10,1280]{2,1,0:T(8,128)(2,1)} %copy.56) | data formatting | bytes 13107200 | tf_op jit(solution)/shard_map/reshape | solution.py:88
  255.6 8.9 %multiply_reduce_fusion = (bf16[2560]{0:T(1024)(128)(2,1)S(1)}, bf16[2560,320]{0,1:T(8,128)(2,1)S(1)}) fusion(f32[2560,320]{0,1:T(8,128)} %fusion.15, f32[2560]{0:T(1024)S(1)} %add_divide_fusion, bf16[2560,1280]{1,0:T(8,128)(2,1)} %reshape.188, bf16[1,320,1280]{2,1,0:T(8,128)(2,1)S(1)} %copy-done.14), kind=kOutput, calls=%fused_computation.16 | convolution fusion | flops 2117629440 | bytes 12303360 | tf_op jit(solution)/shard_map/dot_general | solution.py:46
  264.6 5.6 convolution_convert_fusion
  271.4 7.0 %all-reduce = bf16[4,640]{1,0:T(4,128)(2,1)S(1)} all-reduce(bf16[4,640]{1,0:T(4,128)(2,1)S(1)} %convert_element_type.107), channel_id=5, replica_groups=mesh['expert'=64,'dp'=4] {'dp'}, use_global_device_ids=true, to_apply=%region_9.10.clone | all-reduce | flops 2560 | bytes 10240
  279.9 13.2 %all-to-all-start.3 = ((bf16[64,1,10]{2,1,0:T(2,128)(2,1)}), bf16[64,1,10]{2,1,0:T(2,128)(2,1)S(1)}, u32[]{:S(2)}, u32[]{:S(2)}) async-start(bf16[64,1,10]{2,1,0:T(2,128)(2,1)} %convert_element_type.119), calls=%async_computation.4 | async-start | bytes 65536 | tf_op jit(solution)/shard_map/all_to_all | solution.py:112
  293.1 46.7 %reduce-scatter.2.cloned.1.call-done = bf16[1,640,1280]{2,1,0:T(8,128)(2,1)} async-done(((bf16[4,640,1280]{2,1,0:T(8,128)(2,1)}), bf16[1,640,1280]{2,1,0:T(8,128)(2,1)}) %reduce-scatter.2.cloned.1.call-update) | async-done | bytes 1638416 | tf_op jit(solution)/shard_map/reduce_scatter | solution.py:91
  339.8 4.0 convert_element_type.103
  344.4 10.7 %all-to-all-start.2 = ((bf16[64,10,1280]{2,1,0:T(8,128)(2,1)}), bf16[64,10,1280]{2,1,0:T(8,128)(2,1)S(1)}, u32[]{:S(2)}, u32[]{:S(2)}) async-start(bf16[64,10,1280]{2,1,0:T(8,128)(2,1)} %convert_element_type.103), calls=%async_computation.3 | async-start | bytes 5242880 | tf_op jit(solution)/shard_map/all_to_all | solution.py:109
  357.7 1.4 copy.51
  360.9 6.7 %fusion.10 = bf16[1,1280,320]{1,2,0:T(8,128)(2,1)} fusion(bf16[2560,320]{0,1:T(8,128)(2,1)} %copy-done.15, bf16[2560,1280]{1,0:T(8,128)(2,1)} %reshape.183), kind=kOutput, calls=%fused_computation.22 | convolution fusion | flops 2097561600 | bytes 9011200 | tf_op jit(solution)/shard_map/dot_general | solution.py:51
  367.6 6.9 %fusion.11 = bf16[1,320,1280]{2,1,0:T(8,128)(2,1)} fusion(bf16[2560,1280]{1,0:T(8,128)(2,1)} %reshape.188, f32[2560]{0:T(1024)S(1)} %add_divide_fusion, f32[2560,320]{0,1:T(8,128)S(1)} %copy-done.17), kind=kOutput, calls=%fused_computation.23 | convolution fusion | flops 2114764800 | bytes 10659840 | tf_op jit(solution)/shard_map/dot_general | solution.py:50
  376.1 2.2 gather_fusion.1
  382.7 1.9 fusion.42
  384.6 31.6 %all-to-all-done.2 = bf16[64,10,1280]{2,1,0:T(8,128)(2,1)S(1)} async-done(((bf16[64,10,1280]{2,1,0:T(8,128)(2,1)}), bf16[64,10,1280]{2,1,0:T(8,128)(2,1)S(1)}, u32[]{:S(2)}, u32[]{:S(2)}) %all-to-all-start.2) | async-done | bytes 1638432 | tf_op jit(solution)/shard_map/all_to_all | solution.py:109
  416.2 2.0 convert_reduce_fusion
  418.2 1.9 reshape.191
  420.1 2.2 gather_fusion
  422.3 2.1 gather.13
  424.5 1.7 select_reduce_fusion
  428.0 75.6 %psum.15 = f32[1280]{0:T(1024)} all-reduce(f32[1280]{0:T(1024)S(1)} %get-tuple-element.5), channel_id=1, replica_groups=mesh['expert'=64,'dp'=4] {'expert','dp'}, use_global_device_ids=true, to_apply=%region_17.18 | all-reduce | flops 1280 | bytes 10240 | tf_op jit(solution)/shard_map/psum | solution.py:131
  503.6 130.3 %all-reduce.3.cloned.1.call-done = f32[1280,32]{0,1:T(8,128)} async-done(((f32[1280,32]{0,1:T(8,128)}), f32[1280,32]{0,1:T(8,128)}) %all-reduce.3.cloned.1.call-update) | async-done | bytes 163856 | tf_op jit(solution)/shard_map/psum | solution.py:131
  634.0 1.6 copy.69
  (95 shorter events, 24.9 us)
Async XLA Ops:
  7.2 186.0 %copy-start = (bf16[1,1280,320]{1,2,0:T(8,128)(2,1)S(1)}, bf16[1,1280,320]{1,2,0:T(8,128)(2,1)}, u32[]{:S(2)}) copy-start(bf16[1,1280,320]{1,2,0:T(8,128)(2,1)} %param.11) | copy-start | bytes 2457604
  7.2 156.7 %all-gather.5.cloned.1.call-start = ((), (), s32[]{:S(2)}) async-start(), calls=%async_computation.7 | async-start | bytes 8192000 | tf_op jit(solution)/shard_map/all_gather | solution.py:84
  11.6 3.3 copy-start.12
  12.9 0.7 copy-start.3
  90.8 1.7 copy-start.4
  92.5 139.5 %all-gather.7.cloned.1.call-start = ((), (), s32[]{:S(2)}) async-start(), calls=%async_computation.8 | async-start | bytes 8192000 | tf_op jit(solution)/shard_map/all_gather | solution.py:85
  163.8 176.0 %reduce-scatter.2.cloned.1.call-start = ((), (), s32[]{:S(2)}) async-start(), calls=%async_computation.5 | async-start | bytes 8192000 | tf_op jit(solution)/shard_map/reduce_scatter | solution.py:91
  175.2 13.0 %copy-start.6 = (bf16[1280,32]{0,1:T(8,128)(2,1)S(1)}, bf16[1280,32]{0,1:T(8,128)(2,1)}, u32[]{:S(2)}) copy-start(bf16[1280,32]{0,1:T(8,128)(2,1)} %param.9) | copy-start | bytes 245764
  188.2 5.0 copy-start.1
  242.8 12.8 %copy-start.14 = (bf16[1,320,1280]{2,1,0:T(8,128)(2,1)S(1)}, bf16[1,320,1280]{2,1,0:T(8,128)(2,1)}, u32[]{:S(2)}) copy-start(bf16[1,320,1280]{2,1,0:T(8,128)(2,1)} %param.12) | copy-start | bytes 2457604
  264.6 5.6 copy-start.15
  270.1 0.7 copy-start.16
  279.9 63.9 %all-to-all-start.3 = ((bf16[64,1,10]{2,1,0:T(2,128)(2,1)}), bf16[64,1,10]{2,1,0:T(2,128)(2,1)S(1)}, u32[]{:S(2)}, u32[]{:S(2)}) async-start(bf16[64,1,10]{2,1,0:T(2,128)(2,1)} %convert_element_type.119), calls=%async_computation.4 | async-start | bytes 65536 | tf_op jit(solution)/shard_map/all_to_all | solution.py:112
  343.8 12.2 %copy-start.11 = (s32[128,2]{0,1:T(2,128)S(1)}, s32[128,2]{0,1:T(2,128)}, u32[]{:S(2)}) copy-start(s32[128,2]{0,1:T(2,128)} %param.10) | copy-start | bytes 3076
  343.8 0.6 copy-start.7
  344.4 71.8 %all-to-all-start.2 = ((bf16[64,10,1280]{2,1,0:T(8,128)(2,1)}), bf16[64,10,1280]{2,1,0:T(8,128)(2,1)S(1)}, u32[]{:S(2)}, u32[]{:S(2)}) async-start(bf16[64,10,1280]{2,1,0:T(8,128)(2,1)} %convert_element_type.103), calls=%async_computation.3 | async-start | bytes 5242880 | tf_op jit(solution)/shard_map/all_to_all | solution.py:109
  355.1 278.8 %all-reduce.3.cloned.1.call-start = ((), (), s32[]{:S(2)}) async-start(), calls=%async_computation.6 | async-start | bytes 327680 | tf_op jit(solution)/shard_map/psum | solution.py:131
  360.9 6.7 %copy-start.17 = (f32[2560,320]{0,1:T(8,128)S(1)}, f32[2560,320]{0,1:T(8,128)}, u32[]{:S(2)}) copy-start(f32[2560,320]{0,1:T(8,128)} %fusion.15) | copy-start | bytes 9830404
  367.6 6.9 %copy-start.8 = (bf16[64,1,10]{2,1,0:T(2,128)(2,1)S(1)}, bf16[64,1,10]{2,1,0:T(2,128)(2,1)}, u32[]{:S(2)}) copy-start(bf16[64,1,10]{2,1,0:T(2,128)(2,1)} %copy-done.7) | copy-start | bytes 3844
  420.1 4.4 copy-start.10
  422.3 3.9 copy-start.2
  422.3 3.9 copy-start.9
  422.3 3.9 copy-start.13
  422.3 4.6 copy-start.5
Sparse Core Ops, SparseCore 0:
  92.6 66.4 all-gather.4
  164.0 67.9 all-gather.6
  270.3 69.4 reduce-scatter.1
  384.7 249.2 all-reduce.2
where the time goes:
time: 644 us; the launch traced here: 642 us
  waiting for transfers between devices  243 us (38%)
  blocking collectives  226 us (35%)
  local copies, waits for them, and re-layouts  79.3 us (12%)
  matrix products  41.6 us (6%)
  starting transfers between devices  24.1 us (4%)
  between operations  14.1 us (2%)
  other arithmetic  13.1 us (2%)
    psum x1, waiting for transfers between devices, body(): lax.psum((router_term, gain_product), ('expert', 'dp'))  130 us
    all_to_all x1, blocking collectives, body(): lax.all_to_all(send_m, 'expert', split_axis=0, concat_axis=0, tiled=True)  75.7 us
    psum x1, blocking collectives, body(): lax.psum((router_term, gain_product), ('expert', 'dp'))  75.6 us
    all_to_all x1, blocking collectives, body(): lax.all_to_all(send_d, 'expert', split_axis=0, concat_axis=0, tiled=True)  68.1 us
    reduce_scatter x1, waiting for transfers between devices, body(): lax.psum_scatter(row_gradient.reshape(groups, halves * expert_capacity, w...  46.7 us
    all_gather x1, waiting for transfers between devices, body(): lax.all_gather(recv_d[None], 'dp', axis=0, tiled=True)  34.7 us
    all_to_all x1, waiting for transfers between devices, body(): lax.all_to_all(back_rows.astype(jnp.bfloat16), 'expert', split_axis=0, co...  31.6 us
    all_to_all x1, starting transfers between devices, body(): lax.all_to_all(back_gate.astype(jnp.bfloat16), 'expert', split_axis=0, co...  13.2 us
  transfers between devices with their start and end apart: 6, of which 4 were waited for; matrix products, arithmetic and copies ran while one was open for 13% of the time, Pallas kernels for 0%

commit v1 on v0

--- a/solution.py
+++ b/solution.py
@@ -3,6 +3,24 @@
 import jax.numpy as jnp
 from jax import lax
 from jax.sharding import PartitionSpec as P
+
+
+def gather_around(value, axis, dim):
+    ways, here, turn = (lax.axis_size(axis), lax.axis_index(axis), value.shape[dim])
+    lengths = [n * ways if d == dim else n for d, n in enumerate(value.shape)]
+    full = lax.dynamic_update_slice_in_dim(
+        jnp.zeros(lengths, value.dtype), value, here * turn, axis=dim
+    )
+    going_up = going_down = value
+    for far in range(1, ways // 2 + 1):
+        going_up = lax.ppermute(going_up, axis, [(d, (d + 1) % ways) for d in range(ways)])
+        full = lax.dynamic_update_slice_in_dim(full, going_up, (here - far) % ways * turn, axis=dim)
+        if 2 * far < ways:
+            going_down = lax.ppermute(going_down, axis, [(d, (d - 1) % ways) for d in range(ways)])
+            full = lax.dynamic_update_slice_in_dim(
+                full, going_down, (here + far) % ways * turn, axis=dim
+            )
+    return full
 
 
 def gelu_parts(pre):
@@ -82,7 +100,7 @@
     column = lax.dynamic_slice_in_dim(router, own, 1, 1)
     all_m, all_d = (
         lax.all_gather(recv_m[None], "dp", axis=0, tiled=True),
-        lax.all_gather(recv_d[None], "dp", axis=0, tiled=True),
+        gather_around(recv_d[None], "dp", 0),
     )
     row_gradient, gate_gradient, grad_first, grad_second = expert_pass(
         all_m.reshape(-1, width), all_d.reshape(-1, width), column, w_in[0], w_out[0]

time: 644 us -> 683 us (1.061)
  waiting for transfers between devices: 243 us -> 268 us
  starting transfers between devices: 24.1 us -> 33.4 us
  matrix products: 41.6 us -> 34.7 us
    ppermute x0 -> x3, waiting for transfers between devices: none -> 59.2 us  [the longest x2 59.2 us: gather_around(): lax.ppermute(going_up, axis, [(d, (d + 1) % ways) for d in range(ways)])]
    all_gather x1 -> x0, waiting for transfers between devices: 34.7 us -> none  [body(): lax.all_gather(recv_d[None], 'dp', axis=0, tiled=True)]
    ppermute x0 -> x3, starting transfers between devices: none -> 13.6 us  [the longest x2 12.2 us: gather_around(): lax.ppermute(going_up, axis, [(d, (d + 1) % ways) for d in range(ways)])]
    dynamic_update_slice x0 -> x4, local copies, waits for them, and re-layouts: none -> 12 us  [the longest x2 6.38 us: gather_around(): lax.dynamic_update_slice_in_dim(full, going_up, (here - far) % ways * tur...]
    all_gather x1 -> x0, local copies, waits for them, and re-layouts: 10.8 us -> none  [body(): lax.all_gather(recv_d[None], 'dp', axis=0, tiled=True)]
  transfers between devices with their start and end apart: 6 -> 8, of which waited for: 4 -> 5; matrix products, arithmetic and copies ran while one was open for 13% -> 12% of each run, Pallas kernels for 0% -> 0%
where the time goes in v1:
time: 683 us; the launch traced here: 675 us
  waiting for transfers between devices  268 us (39%)
  blocking collectives  225 us (33%)
  local copies, waits for them, and re-layouts  85.6 us (13%)
  matrix products  34.7 us (5%)
  starting transfers between devices  33.4 us (5%)
  between operations  14.6 us (2%)
  other arithmetic  13.2 us (2%)
    psum x1, waiting for transfers between devices, body(): lax.psum((router_term, gain_product), ('expert', 'dp'))  131 us
    all_to_all x1, blocking collectives, body(): lax.all_to_all(send_m, 'expert', split_axis=0, concat_axis=0, tiled=True)  75.7 us
    psum x1, blocking collectives, body(): lax.psum((router_term, gain_product), ('expert', 'dp'))  75.4 us
    all_to_all x1, blocking collectives, body(): lax.all_to_all(send_d, 'expert', split_axis=0, concat_axis=0, tiled=True)  68.1 us
    ppermute x2, waiting for transfers between devices, gather_around(): lax.ppermute(going_up, axis, [(d, (d + 1) % ways) for d in range(ways)])  59.2 us
    reduce_scatter x1, waiting for transfers between devices, body(): lax.psum_scatter(row_gradient.reshape(groups, halves * expert_capacity, w...  46.5 us
    all_to_all x1, waiting for transfers between devices, body(): lax.all_to_all(back_rows.astype(jnp.bfloat16), 'expert', split_axis=0, co...  31.8 us
  transfers between devices with their start and end apart: 8, of which 5 were waited for; matrix products, arithmetic and copies ran while one was open for 12% of the time, Pallas kernels for 0%

profile of v1, /device:TPU:1, one launch (start us, length us, event | category | flops | bytes accessed | tf_op | source)
XLA Modules:
  0.0 674.9 jit_solution(5699666792328404677)
XLA Ops:
  15.1 75.7 %all_to_all.21 = bf16[64,10,1280]{2,1,0:T(8,128)(2,1)S(1)} all-to-all(bf16[64,10,1280]{2,1,0:T(8,128)(2,1)S(1)} %bitcast.63), channel_id=1, replica_groups=mesh['expert'=64,'dp'=4] {'expert'}, dimensions={0} | all-to-all | bytes 3276800 | tf_op jit(solution)/shard_map/all_to_all | solution.py:96
  94.1 68.1 %all_to_all.22 = bf16[64,10,1280]{2,1,0:T(8,128)(2,1)S(1)} all-to-all(bf16[64,10,1280]{2,1,0:T(8,128)(2,1)S(1)} %bitcast.64), channel_id=1, replica_groups=mesh['expert'=64,'dp'=4] {'expert'}, dimensions={0} | all-to-all | bytes 3276800 | tf_op jit(solution)/shard_map/all_to_all | solution.py:97
  166.5 35.9 %collective-permute-done = bf16[1,64,10,1280]{3,1,2,0:T(8,128)(2,1)} collective-permute-done((bf16[1,64,10,1280]{3,1,2,0:T(8,128)(2,1)}, bf16[1,64,10,1280]{3,1,2,0:T(8,128)(2,1)}, u32[]{:S(2)}, u32[]{:S(2)}) %collective-permute-start) | collective-permute-done | bytes 1638432 | tf_op jit(solution)/shard_map/ppermute | solution.py:16
  202.4 11.0 %collective-permute-start.2 = (bf16[1,64,10,1280]{3,1,2,0:T(8,128)(2,1)}, bf16[1,64,10,1280]{3,1,2,0:T(8,128)(2,1)S(1)}, u32[]{:S(2)}, u32[]{:S(2)}) collective-permute-start(bf16[1,64,10,1280]{3,1,2,0:T(8,128)(2,1)} %collective-permute-done), channel_id=1, source_target_pairs={{0,1},{1,2},{2,3},{3,0},{4,5},{5,6},{6,7},{7,4},{8,9},{9,10},{10,1... | collective-permute-start | bytes 4915208 | tf_op jit(solution)/shard_map/ppermute | solution.py:16
  213.4 4.8 broadcast_in_dim.58
  219.9 3.9 copy_dynamic-update-slice_fusion.2
  223.8 3.9 copy_dynamic-update-slice_fusion.1
  227.7 23.3 %collective-permute-done.2 = bf16[1,64,10,1280]{3,1,2,0:T(8,128)(2,1)S(1)} collective-permute-done((bf16[1,64,10,1280]{3,1,2,0:T(8,128)(2,1)}, bf16[1,64,10,1280]{3,1,2,0:T(8,128)(2,1)S(1)}, u32[]{:S(2)}, u32[]{:S(2)}) %collective-permute-start.2) | collective-permute-done | bytes 1638432 | tf_op jit(solution)/shard_map/ppermute | solution.py:16
  251.0 2.4 copy_dynamic-update-slice_fusion
  253.4 12.8 %reshape.188 = bf16[2560,1280]{1,0:T(8,128)(2,1)} reshape(bf16[4,64,10,1280]{3,2,1,0:T(8,128)(2,1)} %copy_dynamic-update-slice_fusion) | data formatting | bytes 13107200 | tf_op jit(solution)/shard_map/reshape | solution.py:106
  266.2 10.8 %copy.60 = bf16[256,10,1280]{2,1,0:T(8,128)(2,1)} copy(bf16[256,10,1280]{2,0,1:T(8,128)(2,1)} %all-gather.3.cloned.1.call-done) | data formatting | bytes 13107200 | tf_op jit(solution)/shard_map/all_gather | solution.py:102
  277.0 12.8 %reshape.183 = bf16[2560,1280]{1,0:T(8,128)(2,1)} reshape(bf16[256,10,1280]{2,1,0:T(8,128)(2,1)} %copy.60) | data formatting | bytes 13107200 | tf_op jit(solution)/shard_map/reshape | solution.py:106
  289.9 4.8 convolution_reduce_fusion
  294.8 2.3 fusion.15
  297.1 4.0 multiply_reduce_fusion
  302.3 5.5 convolution_convert_fusion
  309.1 6.2 all-reduce
  316.7 8.8 %all-to-all-start.3 = ((bf16[64,1,10]{2,1,0:T(2,128)(2,1)}), bf16[64,1,10]{2,1,0:T(2,128)(2,1)S(1)}, u32[]{:S(2)}, u32[]{:S(2)}) async-start(bf16[64,1,10]{2,1,0:T(2,128)(2,1)} %convert_element_type.119), calls=%async_computation.4 | async-start | bytes 65536 | tf_op jit(solution)/shard_map/all_to_all | solution.py:130
  325.6 46.5 %reduce-scatter.2.cloned.1.call-done = bf16[1,640,1280]{2,1,0:T(8,128)(2,1)} async-done(((bf16[4,640,1280]{2,1,0:T(8,128)(2,1)}), bf16[1,640,1280]{2,1,0:T(8,128)(2,1)}) %reduce-scatter.2.cloned.1.call-update) | async-done | bytes 1638416 | tf_op jit(solution)/shard_map/reduce_scatter | solution.py:109
  372.0 4.0 convert_element_type.103
  376.6 10.8 %all-to-all-start.2 = ((bf16[64,10,1280]{2,1,0:T(8,128)(2,1)}), bf16[64,10,1280]{2,1,0:T(8,128)(2,1)S(1)}, u32[]{:S(2)}, u32[]{:S(2)}) async-start(bf16[64,10,1280]{2,1,0:T(8,128)(2,1)} %convert_element_type.103), calls=%async_computation.3 | async-start | bytes 5242880 | tf_op jit(solution)/shard_map/all_to_all | solution.py:127
  393.3 6.7 fusion.10
  400.0 6.9 %fusion.11 = bf16[1,320,1280]{2,1,0:T(8,128)(2,1)} fusion(bf16[2560,1280]{1,0:T(8,128)(2,1)} %reshape.188, f32[2560]{0:T(1024)S(1)} %add_divide_fusion, f32[2560,320]{0,1:T(8,128)S(1)} %copy-done.18), kind=kOutput, calls=%fused_computation.26 | convolution fusion | flops 2114764800 | bytes 10659840 | tf_op jit(solution)/shard_map/dot_general | solution.py:68
  408.5 1.9 gather_fusion.1
  414.8 1.9 fusion.42
  416.7 31.8 %all-to-all-done.2 = bf16[64,10,1280]{2,1,0:T(8,128)(2,1)S(1)} async-done(((bf16[64,10,1280]{2,1,0:T(8,128)(2,1)}), bf16[64,10,1280]{2,1,0:T(8,128)(2,1)S(1)}, u32[]{:S(2)}, u32[]{:S(2)}) %all-to-all-start.2) | async-done | bytes 1638432 | tf_op jit(solution)/shard_map/all_to_all | solution.py:127
  448.5 2.0 convert_reduce_fusion
  450.5 1.9 reshape.191
  452.4 2.2 gather_fusion
  454.6 2.1 gather.13
  460.3 75.4 %psum.15 = f32[1280]{0:T(1024)} all-reduce(f32[1280]{0:T(1024)S(1)} %get-tuple-element.5), channel_id=1, replica_groups=mesh['expert'=64,'dp'=4] {'expert','dp'}, use_global_device_ids=true, to_apply=%region_17.18 | all-reduce | flops 1280 | bytes 10240 | tf_op jit(solution)/shard_map/psum | solution.py:149
  535.7 130.7 %all-reduce.3.cloned.1.call-done = f32[1280,32]{0,1:T(8,128)} async-done(((f32[1280,32]{0,1:T(8,128)}), f32[1280,32]{0,1:T(8,128)}) %all-reduce.3.cloned.1.call-update) | async-done | bytes 163856 | tf_op jit(solution)/shard_map/psum | solution.py:149
  (109 shorter events, 38.5 us)
Async XLA Ops:
  7.2 287.6 %copy-start = (bf16[1,1280,320]{1,2,0:T(8,128)(2,1)S(1)}, bf16[1,1280,320]{1,2,0:T(8,128)(2,1)}, u32[]{:S(2)}) copy-start(bf16[1,1280,320]{1,2,0:T(8,128)(2,1)} %param.11) | copy-start | bytes 2457604
  7.2 259.0 %all-gather.3.cloned.1.call-start = ((), (), s32[]{:S(2)}) async-start(), calls=%async_computation.7 | async-start | bytes 8192000 | tf_op jit(solution)/shard_map/all_gather | solution.py:102
  11.6 3.3 copy-start.12
  12.9 0.7 copy-start.3
  90.8 1.7 copy-start.4
  92.5 279.6 %reduce-scatter.2.cloned.1.call-start = ((), (), s32[]{:S(2)}) async-start(), calls=%async_computation.5 | async-start | bytes 8192000 | tf_op jit(solution)/shard_map/reduce_scatter | solution.py:109
  163.8 38.6 %collective-permute-start = (bf16[1,64,10,1280]{3,1,2,0:T(8,128)(2,1)}, bf16[1,64,10,1280]{3,1,2,0:T(8,128)(2,1)}, u32[]{:S(2)}, u32[]{:S(2)}) collective-permute-start(bf16[1,64,10,1280]{3,1,2,0:T(8,128)(2,1)} %copy.61), channel_id=1, source_target_pairs={{0,1},{1,2},{2,3},{3,0},{4,5},{5,6},{6,7},{7,4},{8,9},{9,10},{10,1... | collective-permute-start | bytes 4915208 | tf_op jit(solution)/shard_map/ppermute | solution.py:16
  165.0 58.8 %collective-permute-start.1 = (bf16[1,64,10,1280]{3,1,2,0:T(8,128)(2,1)}, bf16[1,64,10,1280]{3,1,2,0:T(8,128)(2,1)}, u32[]{:S(2)}, u32[]{:S(2)}) collective-permute-start(bf16[1,64,10,1280]{3,1,2,0:T(8,128)(2,1)} %copy.61), channel_id=1, source_target_pairs={{0,3},{1,0},{2,1},{3,2},{4,7},{5,4},{6,5},{7,6},{8,11},{9,8},{10,9... | collective-permute-start | bytes 4915208 | tf_op jit(solution)/shard_map/ppermute | solution.py:19
  202.4 48.6 %collective-permute-start.2 = (bf16[1,64,10,1280]{3,1,2,0:T(8,128)(2,1)}, bf16[1,64,10,1280]{3,1,2,0:T(8,128)(2,1)S(1)}, u32[]{:S(2)}, u32[]{:S(2)}) collective-permute-start(bf16[1,64,10,1280]{3,1,2,0:T(8,128)(2,1)} %collective-permute-done), channel_id=1, source_target_pairs={{0,1},{1,2},{2,3},{3,0},{4,5},{5,6},{6,7},{7,4},{8,9},{9,10},{10,1... | collective-permute-start | bytes 4915208 | tf_op jit(solution)/shard_map/ppermute | solution.py:16
  277.0 12.8 %copy-start.6 = (bf16[1280,32]{0,1:T(8,128)(2,1)S(1)}, bf16[1280,32]{0,1:T(8,128)(2,1)}, u32[]{:S(2)}) copy-start(bf16[1280,32]{0,1:T(8,128)(2,1)} %param.9) | copy-start | bytes 245764
  289.9 4.9 copy-start.1
  289.9 7.2 %slice-start = ((s8[6553600]{0:T(1024)(128)(4,1)}), s8[4194304]{0:T(1024)(128)(4,1)S(1)}, s32[]{:S(2)}) async-start(s8[6553600]{0:T(1024)(128)(4,1)} %bitcast.65), calls=%async_computation.8 | async-start | bytes 8388608
  294.7 2.4 slice-start.1
  294.8 2.4 copy-start.14
  297.1 4.0 copy-start.17
  301.1 1.2 copy-start.15
  307.8 0.7 copy-start.16
  316.7 59.3 %all-to-all-start.3 = ((bf16[64,1,10]{2,1,0:T(2,128)(2,1)}), bf16[64,1,10]{2,1,0:T(2,128)(2,1)S(1)}, u32[]{:S(2)}, u32[]{:S(2)}) async-start(bf16[64,1,10]{2,1,0:T(2,128)(2,1)} %convert_element_type.119), calls=%async_computation.4 | async-start | bytes 65536 | tf_op jit(solution)/shard_map/all_to_all | solution.py:130
  376.0 12.3 %copy-start.11 = (s32[128,2]{0,1:T(2,128)S(1)}, s32[128,2]{0,1:T(2,128)}, u32[]{:S(2)}) copy-start(s32[128,2]{0,1:T(2,128)} %param.10) | copy-start | bytes 3076
  376.0 0.6 copy-start.7
  376.6 71.9 %all-to-all-start.2 = ((bf16[64,10,1280]{2,1,0:T(8,128)(2,1)}), bf16[64,10,1280]{2,1,0:T(8,128)(2,1)S(1)}, u32[]{:S(2)}, u32[]{:S(2)}) async-start(bf16[64,10,1280]{2,1,0:T(8,128)(2,1)} %convert_element_type.103), calls=%async_computation.3 | async-start | bytes 5242880 | tf_op jit(solution)/shard_map/all_to_all | solution.py:127
  387.5 279.0 %all-reduce.3.cloned.1.call-start = ((), (), s32[]{:S(2)}) async-start(), calls=%async_computation.6 | async-start | bytes 327680 | tf_op jit(solution)/shard_map/psum | solution.py:149
  393.3 6.7 copy-start.18
  400.0 6.9 %copy-start.8 = (bf16[64,1,10]{2,1,0:T(2,128)(2,1)S(1)}, bf16[64,1,10]{2,1,0:T(2,128)(2,1)}, u32[]{:S(2)}) copy-start(bf16[64,1,10]{2,1,0:T(2,128)(2,1)} %copy-done.7) | copy-start | bytes 3844
  452.4 4.4 copy-start.10
  454.6 3.9 copy-start.2
  454.6 3.9 copy-start.9
  454.6 3.9 copy-start.13
  454.6 4.6 copy-start.5
Sparse Core Ops, SparseCore 0:
  92.6 66.4 all-gather.2
  308.0 64.0 reduce-scatter.1
  416.9 249.5 all-reduce.2
